TPU v7x, 128 devices: a whole 4x4x4 slice. The times are simulated.
128 devices in a mesh: sec: 16 (over y, x_hi, core), lane: 8 (over z, x_lo).
Axes of the slice: x: 4 (x_hi: 2, x_lo: 2; x = x_hi * 2 + x_lo), y: 4, z: 4, core: 2. Of those that a mesh axis runs over, the one named last changes fastest.
Arguments:
- queries: bfloat16 [16, 384, 5120], P('sec', None, 'lane'), may hold values from -40 to 40
- key_value: bfloat16 [4096, 2, 1024], P('sec', None, 'lane'), may hold values from -6 to 6
- grad_out: bfloat16 [16, 384, 5120], P('sec', None, 'lane'), may hold values from -12 to 12
- inputs: bfloat16 [4096, 5120], P('sec'), may hold values from -6 to 6
- w_kv: bfloat16 [5120, 2, 1024], P('sec'), may hold values from -0.078125 to 0.078125
Outputs:
- grad_queries: bfloat16 [16, 384, 5120], P('sec', None, 'lane')
- grad_inputs: bfloat16 [4096, 5120], P(('sec', 'lane'))
- grad_w_kv: float32 [5120, 2, 1024], P('sec', None, 'lane')
All inputs are finite; a program needn't handle non-finite values.
Results may differ from a plain program's by a relative error of at most 0.0058.
Values may be sent and summed in bfloat16 or wider, within the bound.
A program may use at most 128 MiB of HBM per device.

v0:
```python
import math

import jax
import jax.numpy as jnp
from jax import lax
from jax.sharding import PartitionSpec as P

NQH = 40
KVH = 8
HD = 128


def attend(q_rows, do_rows, k_head, v_head, last_key, block_count, softmax_scale):
    block_size = k_head.shape[0] // block_count
    k_blocks = k_head.reshape(block_count, block_size, k_head.shape[1])
    v_blocks = v_head.reshape(block_count, block_size, v_head.shape[1])
    offsets = jnp.arange(block_count, dtype=jnp.int32) * block_size
    row_count = q_rows.shape[0]

    def scores(k_block, offset):
        raw = jnp.dot(q_rows, k_block.T, preferred_element_type=jnp.float32) * softmax_scale
        visible = (offset + jnp.arange(block_size, dtype=jnp.int32))[None, :] <= last_key[:, None]
        return (raw, visible)

    def stats_step(carry, items):
        run_max, run_sum, run_dot = carry
        k_block, v_block, offset = items
        raw, visible = scores(k_block, offset)
        dprobs = jnp.dot(do_rows, v_block.T, preferred_element_type=jnp.float32)
        masked = jnp.where(visible, raw, -jnp.inf)
        new_max = jnp.maximum(run_max, jnp.max(masked, axis=1))
        factor = jnp.exp(run_max - new_max)
        weights = jnp.exp(masked - new_max[:, None])
        run_sum = run_sum * factor + jnp.sum(weights, axis=1)
        run_dot = run_dot * factor + jnp.sum(weights * dprobs, axis=1)
        return ((new_max, run_sum, run_dot), None)

    start_max = jnp.full((row_count,), -1e30, jnp.float32)
    start_zero = jnp.zeros((row_count,), jnp.float32)
    (run_max, run_sum, run_dot), _ = lax.scan(
        stats_step, (start_max, start_zero, start_zero), (k_blocks, v_blocks, offsets)
    )
    lse = run_max + jnp.log(run_sum)
    row_delta = run_dot / run_sum

    def grad_step(carry, items):
        k_block, v_block, offset = items
        raw, visible = scores(k_block, offset)
        probs = jnp.where(visible, jnp.exp(raw - lse[:, None]), 0.0)
        dprobs = jnp.dot(do_rows, v_block.T, preferred_element_type=jnp.float32)
        dscores = (probs * (dprobs - row_delta[:, None])).astype(jnp.bfloat16)
        probs_low = probs.astype(jnp.bfloat16)
        contract_rows = (((0,), (0,)), ((), ()))
        dk_block = (
            lax.dot_general(dscores, q_rows, contract_rows, preferred_element_type=jnp.float32)
            * softmax_scale
        )
        dv_block = lax.dot_general(
            probs_low, do_rows, contract_rows, preferred_element_type=jnp.float32
        )
        carry = carry + jnp.dot(dscores, k_block, preferred_element_type=jnp.float32)
        return (carry, (dk_block, dv_block))

    start_dq = jnp.zeros((row_count, k_head.shape[1]), jnp.float32)
    dq_sum, (dk_blocks, dv_blocks) = lax.scan(grad_step, start_dq, (k_blocks, v_blocks, offsets))
    head_dim = k_head.shape[1]
    return (
        dq_sum * softmax_scale,
        dk_blocks.reshape(-1, head_dim),
        dv_blocks.reshape(-1, head_dim),
    )


def local(queries, key_value, grad_out, inputs, w_kv):
    head_dim = HD
    group_size = NQH // KVH
    softmax_scale = head_dim ** (-0.5)
    gathered = lax.all_gather(key_value, "sec", axis=0, tiled=True)
    key_count = gathered.shape[0]
    query_local = queries[0]
    grad_local = grad_out[0]
    query_count = query_local.shape[0]
    block_count = math.gcd(key_count, max(1, key_count // 512))
    last_key = (
        key_count
        - query_count
        + jnp.arange(query_count * group_size, dtype=jnp.int32) // group_size
    )
    q_rows = query_local.reshape(query_count * group_size, head_dim)
    do_rows = grad_local.reshape(query_count * group_size, head_dim)
    k_head = gathered[:, 0, 0:head_dim]
    v_head = gathered[:, 1, 0:head_dim]
    dq_head, dk_head, dv_head = attend(
        q_rows, do_rows, k_head, v_head, last_key, block_count, softmax_scale
    )
    dq_list = dq_head.reshape(query_count, group_size * head_dim)
    grad_queries = dq_list.astype(jnp.bfloat16)[None]
    dkv_part = jnp.stack([dk_head, dv_head], axis=1)
    summed = lax.psum_scatter(dkv_part, "sec", scatter_dimension=0, tiled=True)
    dkv = summed.astype(jnp.bfloat16)
    key_rows = dkv.shape[0]
    flat_grads = dkv.reshape(key_rows, -1)
    contract_first = (((0,), (0,)), ((), ()))
    contract_last = (((1,), (1,)), ((), ()))
    owned_cols = inputs.shape[1] // lax.axis_size("sec")
    term = lax.dot_general(inputs, flat_grads, contract_first, preferred_element_type=jnp.float32)
    grad_w_kv = lax.psum_scatter(
        term.reshape(owned_cols * lax.axis_size("sec"), 2, dkv.shape[2]),
        "sec",
        scatter_dimension=0,
        tiled=True,
    )
    regrouped = lax.all_to_all(dkv, "lane", split_axis=0, concat_axis=2, tiled=True)
    local_flat = regrouped.reshape(regrouped.shape[0], -1)
    w_piece = lax.all_gather(w_kv, "sec", axis=0, tiled=True)
    piece_flat = w_piece.reshape(w_piece.shape[0], -1)
    grad_inputs = lax.dot_general(
        local_flat, piece_flat, contract_last, preferred_element_type=jnp.float32
    ).astype(jnp.bfloat16)
    return (grad_queries, grad_inputs, grad_w_kv)


def solution(mesh):
    in_specs = (
        P("sec", None, "lane"),
        P("sec", None, "lane"),
        P("sec", None, "lane"),
        P("sec", None),
        P("sec", None, None),
    )
    out_specs = (P("sec", None, "lane"), P(("sec", "lane"), None), P("sec", None, "lane"))
    return jax.shard_map(local, mesh=mesh, in_specs=in_specs, out_specs=out_specs, check_vma=False)
```

profile of v0, /device:TPU:1, one launch (start us, length us, event | category | flops | bytes accessed | tf_op | source)
XLA Modules:
  0.0 621.7 jit_solution(14753554372606013544)
XLA Ops:
  9.1 2.2 reshape_squeeze.13
  12.7 49.4 %all-gather.3.cloned.1.call-done = bf16[4096,2,128]{2,0,1:T(8,128)(2,1)} async-done(((bf16[256,2,128]{2,0,1:T(8,128)(2,1)}), bf16[4096,2,128]{2,0,1:T(8,128)(2,1)}) %all-gather.3.cloned.1.call-update) | async-done | bytes 2097168 | tf_op jit(solution)/shard_map/all_gather | solution.py:78
  62.1 3.0 fusion.45
  65.1 43.9 %while.30 = (s32[]{:T(128)}, f32[1920]{0:T(1024)S(1)}, f32[1920]{0:T(1024)S(1)}, f32[1920]{0:T(1024)S(1)}, s32[8]{0:T(128)S(1)}, /*index=5*/bf16[8,512,128]{2,1,...) while((s32[]{:T(128)}, f32[1920]{0:T(1024)S(1)}, ...), condition=%wide.region_4.5_spmd.clone, body=%wide.region_0.4_spmd.clone.sunk | while | flops 512195072 | bytes 13199512 | solution.py:40
  109.0 78.7 %while.31 = (s32[]{:T(128)}, f32[1920,128]{1,0:T(8,128)}, f32[8,512,128]{2,1,0:T(8,128)}, f32[8,512,128]{2,1,0:T(8,128)}, s32[8]{0:T(128)S(1)}, /*index=5*/bf16[...) while((s32[]{:T(128)}, f32[1920,128]{1,0:T(8,128)}, ...), condition=%wide.region_6.7_spmd.clone, body=%wide.region_5.6_spmd.clone.sunk | while | flops 1266730368 | bytes 32409864 | solution.py:65
  110.3 2.1 bitcast_select_fusion.3
  120.1 2.1 bitcast_select_fusion.3
  130.0 2.1 bitcast_select_fusion.3
  139.8 2.1 bitcast_select_fusion.3
  149.6 2.1 bitcast_select_fusion.3
  159.4 2.1 bitcast_select_fusion.3
  179.1 2.1 bitcast_select_fusion.3
  187.7 2.9 copy.26
  190.6 2.9 copy.25
  193.5 4.6 pad_maximum_fusion
  198.2 77.7 %reduce-scatter.2.cloned.1.call-done = f32[256,2,128]{0,2,1:T(8,128)} async-done(((f32[4096,2,128]{0,2,1:T(8,128)}), f32[256,2,128]{0,2,1:T(8,128)}) %reduce-scatter.2.cloned.1.call-update) | async-done | bytes 262160 | tf_op jit(solution)/shard_map/reduce_scatter | solution.py:99
  276.9 3.1 fusion.47
  280.0 8.8 %copy.24 = f32[5120,2,128]{2,1,0:T(2,128)} copy(f32[5120,2,128]{0,2,1:T(8,128)} %bitcast.110) | data formatting | bytes 10485760 | tf_op jit(solution)/shard_map/reshape | solution.py:108
  291.5 4.1 all-to-all-start
  298.0 3.1 all-to-all-done
  301.2 149.6 %all-reduce.3.cloned.1.call-done = f32[5120,2,128]{2,1,0:T(2,128)} async-done(((f32[5120,2,128]{2,1,0:T(2,128)}), f32[5120,2,128]{2,1,0:T(2,128)}) %all-reduce.3.cloned.1.call-update) | async-done | bytes 5242896
  452.6 130.4 %all-gather.5.cloned.1.call-done = bf16[5120,2,1024]{2,1,0:T(2,128)(2,1)} async-done(((bf16[320,2,1024]{2,1,0:T(2,128)(2,1)}), bf16[5120,2,1024]{2,1,0:T(2,128)(2,1)}) %all-gather.5.cloned.1.call-update) | async-done | bytes 20971536 | tf_op jit(solution)/shard_map/all_gather | solution.py:115
  582.9 21.1 %copy.28 = bf16[640,8,2,1024]{3,1,2,0:T(8,128)(2,1)} copy(bf16[640,8,2,1024]{3,2,1,0:T(2,128)(2,1)} %bitcast.109) | data formatting | bytes 41943040
  604.1 11.1 %convolution_convert_fusion = bf16[32,5120]{1,0:T(8,128)(2,1)} fusion(bf16[5120,2048]{1,0:T(8,128)(2,1)} %bitcast.108, bf16[4,8,16,128]{3,2,1,0:T(8,128)(2,1)S(1)} %bitcast.116), kind=kOutput, calls=%fused_computation.57 | convolution fusion | flops 671252480 | bytes 21430272 | tf_op jit(solution)/shard_map/dot_general | solution.py:117
  (207 shorter events, 117.3 us)
Async XLA Ops:
  7.2 269.7 %copy-start = (bf16[256,5120]{1,0:T(8,128)(2,1)S(1)}, bf16[256,5120]{1,0:T(8,128)(2,1)}, u32[]{:S(2)}) copy-start(bf16[256,5120]{1,0:T(8,128)(2,1)} %param.12) | copy-start | bytes 7864324
  7.2 54.9 %all-gather.3.cloned.1.call-start = ((), (), s32[]{:S(2)}) async-start(), calls=%async_computation.2 | async-start | bytes 2228224 | tf_op jit(solution)/shard_map/all_gather | solution.py:78
  9.0 266.9 %reduce-scatter.2.cloned.1.call-start = ((), (), s32[]{:S(2)}) async-start(), calls=%async_computation.3 | async-start | bytes 4456448 | tf_op jit(solution)/shard_map/reduce_scatter | solution.py:99
  114.0 3.4 copy-start.3
  117.5 1.4 copy-start.2
  123.9 1.4 copy-start.1
  123.9 3.4 copy-start.3
  127.3 1.4 copy-start.2
  133.7 3.4 copy-start.3
  143.5 1.4 copy-start.1
  143.5 3.4 copy-start.3
  153.3 3.4 copy-start.3
  156.8 1.4 copy-start.2
  163.2 1.4 copy-start.1
  163.2 3.4 copy-start.3
  166.6 1.4 copy-start.2
  173.0 1.4 copy-start.1
  173.0 3.4 copy-start.3
  176.5 1.4 copy-start.2
  182.9 3.4 copy-start.3
  186.3 1.4 copy-start.2
  198.2 252.7 %all-reduce.3.cloned.1.call-start = ((), (), s32[]{:S(2)}) async-start(), calls=%async_computation.5 | async-start | bytes 10485760
  288.8 294.1 %all-gather.5.cloned.1.call-start = ((), (), s32[]{:S(2)}) async-start(), calls=%async_computation.4 | async-start | bytes 22282240 | tf_op jit(solution)/shard_map/all_gather | solution.py:115
  291.5 9.7 %all-to-all-start = ((bf16[256,2,128]{2,1,0:T(2,128)(2,1)}), bf16[256,2,128]{2,1,0:T(2,128)(2,1)S(1)}, u32[]{:S(2)}, u32[]{:S(2)}) async-start(bf16[256,2,128]{2,1,0:T(2,128)(2,1)} %copy.21), calls=%async_computation.1 | async-start | bytes 262144 | tf_op jit(solution)/shard_map/all_to_all | solution.py:113
  (7 other events, 9.1 us)
Sparse Core Ops, SparseCore 0:
  11.0 51.0 all-gather.2
  198.3 77.5 reduce-scatter.1
  288.9 161.8 all-reduce.2
  453.2 129.7 all-gather.4
where the time goes:
time: 623 us; the launch traced here: 622 us
  waiting for transfers between devices  411 us (66%)
  matrix products  111 us (18%)
  local copies, waits for them, and re-layouts  57.8 us (9%)
  other arithmetic  22.2 us (4%)
  between operations  14.5 us (2%)
    unnamed x5, waiting for transfers between devices  150 us
    all_gather x1, waiting for transfers between devices, local(): w_piece = lax.all_gather(w_kv, 'sec', axis=0, tiled=True)  130 us
    reduce_scatter x1, waiting for transfers between devices, local(): summed = lax.psum_scatter(dkv_part, 'sec', scatter_dimension=0, tiled=True)  77.7 us
    all_gather x1, waiting for transfers between devices, local(): gathered = lax.all_gather(key_value, 'sec', axis=0, tiled=True)  49.4 us
    dot_general x16, matrix products, scores(): jnp.dot(q_rows, k_block.T, preferred_element_type=jnp.float32)  31.3 us
    unnamed x8, local copies, waits for them, and re-layouts  25.2 us
    dot_general x8, matrix products, grad_step(): jnp.dot(dscores, k_block, preferred_element_type=jnp.float32)  16.1 us
    dot_general x8, matrix products, stats_step(): dprobs = jnp.dot(do_rows, v_block.T, preferred_element_type=jnp.float32)  14.1 us
  transfers between devices with their start and end apart: 5, of which 5 were waited for; matrix products, arithmetic and copies ran while one was open for 1% of the time, Pallas kernels for 0%

commit v1 on v0

v1 whole, which is shorter than its diff:
```python
import functools

import jax
import jax.numpy as jnp
from jax import lax
from jax.experimental import pallas as pl
from jax.experimental.pallas import tpu as pltpu
from jax.sharding import PartitionSpec as P

HD = 128
SCALE = HD**-0.5
SCALE_LOG2E = SCALE * 1.4426950408889634
MESH = pl.DeviceIdType.MESH
f32, bf16 = jnp.float32, jnp.bfloat16
NT = (((1,), (1,)), ((), ()))
TN = (((0,), (0,)), ((), ()))
NN = (((1,), (0,)), ((), ()))
dot = functools.partial(lax.dot_general, preferred_element_type=f32)

CHIPS = 8
LANES = 8
ROWS = 256
KEYS = 4096
QL = 384
GROUP = 5
BLK = 256
NBLK = 8
CH = 2048
SUB = 64
DCOL = 640


def kernel(
    q_ref, do_ref, kv_ref, x_ref, w_ref, dq_ref, gi_ref, gw_ref,
    kvall, qs, dos, kT, ebuf, dpbuf, mbuf, acc, psend, precv, rsend, rrecv,
    dall, gin, xall, wall, gsend, gout, term, trecv,
    loc, kv_s, kv_r, kvf_s, kvf_r, x1_s, x1_r, x2_s, x2_r, w_s, w_r,
    p_s, p_r, r_s, r_r, a_s, a_r, g_s, g_r, o_s, o_r, t_s, t_r,
):
    s = lax.axis_index("sec")
    lane = lax.axis_index("lane")
    core = s % 2
    chip = s // 2
    partner = {"sec": chip * 2 + 1 - core, "lane": lane}

    def at_chip(k):
        return {"sec": k * 2 + core, "lane": lane}

    def at_lane(t):
        return {"sec": s, "lane": t}

    def remote(src, dst, ssem, rsem, to):
        return pltpu.make_async_remote_copy(
            src_ref=src, dst_ref=dst, send_sem=ssem, recv_sem=rsem, device_id=to, device_id_type=MESH
        )

    barrier = pltpu.get_barrier_semaphore()
    pl.semaphore_signal(barrier, inc=1, device_id=partner, device_id_type=MESH)
    for d in range(1, 8):
        pl.semaphore_signal(barrier, inc=1, device_id=at_chip((chip + d) % 8), device_id_type=MESH)
        pl.semaphore_signal(barrier, inc=1, device_id=at_lane((lane + d) % 8), device_id_type=MESH)

    local = [
        pltpu.make_async_copy(kv_ref, kvall.at[pl.ds(s * ROWS, ROWS)], loc.at[0]),
        pltpu.make_async_copy(
            x_ref.at[pl.ds(lane * 32, 32), pl.ds(chip * DCOL, DCOL)],
            xall.at[chip, pl.ds(lane * 32, 32)],
            loc.at[1],
        ),
        pltpu.make_async_copy(w_ref, wall.at[pl.ds(core * 320, 320)], loc.at[2]),
    ]
    for copy in local:
        copy.start()
    for h in range(GROUP):
        qs[h * QL : (h + 1) * QL, :] = q_ref[:, h * HD : (h + 1) * HD]
        dos[h * QL : (h + 1) * QL, :] = do_ref[:, h * HD : (h + 1) * HD]
    qs[GROUP * QL :, :] = jnp.zeros((NBLK * BLK - GROUP * QL, HD), bf16)
    dos[GROUP * QL :, :] = jnp.zeros((NBLK * BLK - GROUP * QL, HD), bf16)
    pl.semaphore_wait(barrier, 15)

    mine = kvall.at[pl.ds(s * ROWS, ROWS)]
    kv_out = [
        remote(kv_ref, mine, kv_s.at[d - 1], kv_r.at[d - 1], at_chip((chip + d) % 8)) for d in range(1, 8)
    ]
    kv_fwd = [remote(kv_ref, mine, kvf_s.at[0], kvf_r.at[0], partner)]
    for copy in kv_out + kv_fwd:
        copy.start()
    x_out = [
        remote(
            x_ref.at[pl.ds(lane * 32, 32), pl.ds(((chip + d) % 8) * DCOL, DCOL)],
            xall.at[chip, pl.ds(lane * 32, 32)],
            x1_s.at[d - 1],
            x1_r.at[d - 1],
            at_chip((chip + d) % 8),
        )
        for d in range(1, 8)
    ]
    w_out = remote(w_ref, wall.at[pl.ds(core * 320, 320)], w_s, w_r, partner)
    for copy in x_out:
        copy.start()
    w_out.start()
    for d in range(1, 8):
        kv_out[d - 1].wait_recv()
        part = kvall.at[pl.ds((((chip + 8 - d) % 8) * 2 + core) * ROWS, ROWS)]
        copy = remote(part, part, kvf_s.at[d], kvf_r.at[d], partner)
        copy.start()
        kv_fwd.append(copy)
    local[0].wait()
    local[1].wait()
    for copy in x_out:
        copy.wait_recv()
    rows_here = xall.at[:, pl.ds(lane * 32, 32)]
    x_lane = [
        remote(rows_here, rows_here, x2_s.at[d - 1], x2_r.at[d - 1], at_lane((lane + d) % 8))
        for d in range(1, 8)
    ]
    for copy in x_lane:
        copy.start()
    for copy in kv_fwd:
        copy.wait_recv()

    kT[...] = kvall[:, 0:HD].T

    def block(b, first):
        rows = pl.ds(b * BLK, BLK)
        qb = qs[rows, :]
        dob = dos[rows, :]
        i0 = (b * BLK) % QL

        def stage_a(ch, carry, mask):
            base = ch * CH
            scores = dot(kvall[pl.ds(base, CH), 0:HD], qb, NT)
            dprobs = dot(kvall[pl.ds(base, CH), HD : 2 * HD], dob, NT)
            m, total, dots = carry
            for u in range(CH // SUB):
                sc = scores[u * SUB : (u + 1) * SUB]
                dp = dprobs[u * SUB : (u + 1) * SUB]
                if mask and base + (u + 1) * SUB > KEYS - QL:
                    j = lax.broadcasted_iota(jnp.int32, (SUB, BLK), 0) + (base + u * SUB - (KEYS - QL))
                    i = lax.broadcasted_iota(jnp.int32, (SUB, BLK), 1) + i0
                    i = jnp.where(i >= QL, i - QL, i)
                    sc = jnp.where(j <= i, sc, -1e30)
                sc = sc.reshape(SUB // 8, 8, BLK)
                dp8 = dp.reshape(SUB // 8, 8, BLK)
                top = jnp.max(sc, axis=0) * SCALE_LOG2E
                e = jnp.exp2(sc * SCALE_LOG2E - top[None])
                part = jnp.sum(e, axis=0)
                part_dot = jnp.sum(e * dp8, axis=0)
                ebuf[pl.ds(base + u * SUB, SUB), :] = e.reshape(SUB, BLK)
                dpbuf[pl.ds(base + u * SUB, SUB), :] = dp
                mbuf[ch * (CH // SUB) + u] = top
                new = jnp.maximum(m, top)
                old_f = jnp.exp2(m - new)
                new_f = jnp.exp2(top - new)
                total = total * old_f + part * new_f
                dots = dots * old_f + part_dot * new_f
                m = new
            return m, total, dots

        zero = jnp.zeros((8, BLK), f32)
        carry = (jnp.full((8, BLK), -1e35, f32), zero, zero)
        for ch in range(KEYS // CH):
            carry = stage_a(ch, carry, ch == KEYS // CH - 1)
        m, total, dots = carry
        top = jnp.max(m, axis=0, keepdims=True)
        f = jnp.exp2(m - top)
        inv = 1.0 / jnp.sum(total * f, axis=0, keepdims=True)
        delta = jnp.sum(dots * f, axis=0, keepdims=True) * inv
        delta8 = jnp.broadcast_to(delta, (8, BLK))
        inv8 = jnp.broadcast_to(inv, (8, BLK))
        top8 = jnp.broadcast_to(top, (8, BLK))

        def stage_c(ch, dq):
            base = ch * CH
            probs, dscores = [], []
            for u in range(CH // SUB):
                f = jnp.exp2(mbuf[ch * (CH // SUB) + u] - top8) * inv8
                e = ebuf[pl.ds(base + u * SUB, SUB), :].reshape(SUB // 8, 8, BLK)
                dp = dpbuf[pl.ds(base + u * SUB, SUB), :].reshape(SUB // 8, 8, BLK)
                p = e * f[None]
                probs.append(p.reshape(SUB, BLK).astype(bf16))
                dscores.append((p * (dp - delta8[None])).reshape(SUB, BLK).astype(bf16))
            probs = jnp.concatenate(probs, axis=0)
            dscores = jnp.concatenate(dscores, axis=0)
            dv = dot(probs, dob, NN)
            dk = dot(dscores, qb, NN)
            if first:
                acc[pl.ds(base, CH), 0:HD] = dk
                acc[pl.ds(base, CH), HD : 2 * HD] = dv
            else:
                acc[pl.ds(base, CH), 0:HD] += dk
                acc[pl.ds(base, CH), HD : 2 * HD] += dv
            return dq + dot(kT[:, pl.ds(base, CH)], dscores, NN)

        dq = lax.fori_loop(0, KEYS // CH, stage_c, jnp.zeros((HD, BLK), f32))
        qs[rows, :] = (dq.T * SCALE).astype(bf16)

    block(0, True)

    def body(b, carry):
        block(b, False)
        return carry

    lax.fori_loop(1, NBLK, body, 0)
    for h in range(GROUP):
        dq_ref[:, h * HD : (h + 1) * HD] = qs[h * QL : (h + 1) * QL, :]

    def pair(rows):
        part = acc[rows, :]
        col = lax.broadcasted_iota(jnp.int32, (ROWS, 2 * HD), 1)
        return jnp.where(col < HD, part * SCALE, part)

    p_out = []
    for d in range(1, 9):
        k = (chip + d) % 8
        psend[d - 1] = pair(pl.ds((2 * k + 1 - core) * ROWS, ROWS)).astype(bf16)
        copy = remote(psend.at[d - 1], precv.at[d - 1], p_s.at[d - 1], p_r.at[d - 1], partner)
        copy.start()
        p_out.append(copy)
    r_out = []
    own = None
    for d in range(1, 9):
        k = (chip + d) % 8
        part = pair(pl.ds((2 * k + core) * ROWS, ROWS))
        p_out[d - 1].wait_recv()
        both = part + precv[d - 1].astype(f32)
        if d < 8:
            rsend[d - 1] = both.astype(bf16)
            copy = remote(rsend.at[d - 1], rrecv.at[d - 1], r_s.at[d - 1], r_r.at[d - 1], at_chip(k))
            copy.start()
            r_out.append(copy)
        else:
            own = both
    for d in range(1, 8):
        r_out[d - 1].wait_recv()
        own = own + rrecv[d - 1].astype(f32)
    dall[chip] = own.astype(bf16)

    a_out = [
        remote(dall.at[chip], dall.at[chip], a_s.at[d - 1], a_r.at[d - 1], at_chip((chip + d) % 8))
        for d in range(1, 8)
    ]
    for copy in a_out:
        copy.start()

    def to_lane(k):
        return remote(dall.at[k], gin.at[lane], g_s.at[k], g_r.at[lane], at_lane(k))

    def stay(k):
        return pltpu.make_async_copy(dall.at[k], gin.at[lane], g_r.at[lane])

    def pass_on(k):
        @pl.when(k != lane)
        def _():
            to_lane(k).start()

        @pl.when(k == lane)
        def _():
            stay(k).start()

    pass_on(chip)
    local[2].wait()
    w_out.wait()
    for copy in x_lane:
        copy.wait()
    for d in range(1, 8):
        a_out[d - 1].wait_recv()
        pass_on((chip + 8 - d) % 8)

    total = dot(xall[0], dall[0], TN)
    for k in range(1, 8):
        total = total + dot(xall[k], dall[k], TN)
    term[...] = total
    t_out = remote(term.at[pl.ds((1 - core) * 320, 320)], trecv, t_s, t_r, partner)
    t_out.start()

    for t in range(8):

        @pl.when(t != lane)
        def _():
            remote(dall.at[t], gin.at[t], g_s.at[t], g_r.at[t], at_lane(t)).wait_recv()

        @pl.when(t == lane)
        def _():
            stay(t).wait()

    grads = dot(gin[0], wall[:, 0 : 2 * HD], NT)
    for t in range(1, 8):
        grads = grads + dot(gin[t], wall[:, t * 2 * HD : (t + 1) * 2 * HD], NT)
    gsend[...] = grads.astype(bf16)

    cols = pl.ds(chip * DCOL, DCOL)

    def hand(t):
        return remote(
            gsend.at[pl.ds(t * 32, 32)],
            gout.at[:, cols],
            o_s.at[t],
            o_r.at[chip],
            {"sec": lane * 2 + core, "lane": t},
        )

    def hand_here(t):
        return pltpu.make_async_copy(gsend.at[pl.ds(t * 32, 32)], gout.at[:, cols], o_r.at[chip])

    for t in range(8):
        here = jnp.logical_and(lane == chip, lane == t)

        @pl.when(jnp.logical_not(here))
        def _():
            hand(t).start()

        @pl.when(here)
        def _():
            hand_here(t).start()

    t_out.wait_recv()
    gw_ref[...] = term[pl.ds(core * 320, 320), :] + trecv[...]

    for k in range(8):
        here = jnp.logical_and(lane == chip, k == chip)
        arrived = gout.at[:, pl.ds(k * DCOL, DCOL)]

        @pl.when(jnp.logical_not(here))
        def _():
            remote(
                gsend.at[pl.ds(0, 32)], arrived, o_s.at[k], o_r.at[k], {"sec": k * 2 + core, "lane": chip}
            ).wait_recv()

        @pl.when(here)
        def _():
            pltpu.make_async_copy(gsend.at[pl.ds(0, 32)], arrived, o_r.at[k]).wait()

    gi_ref[...] = gout[...]

    for copy in kv_out + kv_fwd + x_out + p_out + r_out + a_out + [t_out]:
        copy.wait_send()
    for t in range(8):

        @pl.when(t != lane)
        def _():
            remote(dall.at[t], gin.at[lane], g_s.at[t], g_r.at[lane], at_lane(t)).wait_send()

        @pl.when(jnp.logical_not(jnp.logical_and(lane == chip, lane == t)))
        def _():
            hand(t).wait_send()


def local_step(queries, key_value, grad_out, inputs, w_kv):
    kv = key_value.reshape(ROWS, 2 * HD)
    w = w_kv.reshape(320, 2, LANES, HD).transpose(0, 2, 1, 3).reshape(320, 2 * LANES * HD)
    vmem = pltpu.VMEM
    dma = pltpu.SemaphoreType.DMA
    whole = pl.BlockSpec(memory_space=vmem)
    there = pl.BlockSpec(memory_space=pl.ANY)
    blocks = (CHIPS, ROWS, 2 * HD)
    grad_queries, grad_inputs, grad_w = pl.pallas_call(
        kernel,
        out_shape=(
            jax.ShapeDtypeStruct((QL, GROUP * HD), bf16),
            jax.ShapeDtypeStruct((32, CHIPS * DCOL), bf16),
            jax.ShapeDtypeStruct((320, 2 * HD), f32),
        ),
        in_specs=[whole, whole, whole, there, there],
        out_specs=(whole, whole, whole),
        scratch_shapes=[
            vmem((KEYS, 2 * HD), bf16),
            vmem((NBLK * BLK, HD), bf16),
            vmem((NBLK * BLK, HD), bf16),
            vmem((HD, KEYS), bf16),
            vmem((KEYS, BLK), f32),
            vmem((KEYS, BLK), f32),
            vmem((KEYS // SUB, 8, BLK), f32),
            vmem((KEYS, 2 * HD), f32),
            vmem(blocks, bf16),
            vmem(blocks, bf16),
            vmem((7, ROWS, 2 * HD), bf16),
            vmem((7, ROWS, 2 * HD), bf16),
            vmem(blocks, bf16),
            vmem(blocks, bf16),
            vmem((CHIPS, ROWS, DCOL), bf16),
            vmem((DCOL, 2 * LANES * HD), bf16),
            vmem((ROWS, DCOL), bf16),
            vmem((32, CHIPS * DCOL), bf16),
            vmem((DCOL, 2 * HD), f32),
            vmem((320, 2 * HD), f32),
            dma((3,)),
            dma((7,)), dma((7,)), dma((8,)), dma((8,)), dma((7,)), dma((7,)), dma((7,)), dma((7,)), dma, dma,
            dma((8,)), dma((8,)), dma((7,)), dma((7,)), dma((7,)), dma((7,)), dma((8,)), dma((8,)),
            dma((8,)), dma((8,)), dma, dma,
        ],
        compiler_params=pltpu.CompilerParams(
            collective_id=0, has_side_effects=True, vmem_limit_bytes=60 * 2**20
        ),
        name="step",
    )(queries[0], grad_out[0], kv, inputs, w)
    return grad_queries[None], grad_inputs, grad_w.reshape(320, 2, HD)


def solution(mesh):
    in_specs = (
        P("sec", None, "lane"),
        P("sec", None, "lane"),
        P("sec", None, "lane"),
        P("sec", None),
        P("sec", None, None),
    )
    out_specs = (P("sec", None, "lane"), P(("sec", "lane"), None), P("sec", None, "lane"))
    return jax.shard_map(local_step, mesh=mesh, in_specs=in_specs, out_specs=out_specs, check_vma=False)
```

time: 623 us -> 126 us (0.20)
  waiting for transfers between devices: 411 us -> 0 us
  Pallas kernels: 0 us -> 114 us
  matrix products: 111 us -> 0 us
  local copies, waits for them, and re-layouts: 57.8 us -> 10.3 us
  other arithmetic: 22.2 us -> 0 us
  between operations: 14.5 us -> 0.65 us
    all_gather x2 -> x0, waiting for transfers between devices: 180 us -> none  [the longest x1 130 us: local(): w_piece = lax.all_gather(w_kv, 'sec', axis=0, tiled=True)]
    unnamed x5 -> x0, waiting for transfers between devices: 150 us -> none
    pallas_call x0 -> x1, Pallas kernels: none -> 114 us  [local_step(): pl.pallas_call(kernel, out_shape=(jax.ShapeDtypeStruct((QL, GROUP * HD),...]
    dot_general x58 -> x0, matrix products: 111 us -> none  [the longest x16 31.3 us: scores(): jnp.dot(q_rows, k_block.T, preferred_element_type=jnp.float32)]
    reduce_scatter x1 -> x0, waiting for transfers between devices: 77.7 us -> none  [local(): summed = lax.psum_scatter(dkv_part, 'sec', scatter_dimension=0, tiled=True)]
    unnamed x8 -> x5, local copies, waits for them, and re-layouts: 25.2 us -> 4.16 us
    add x40 -> x0, other arithmetic: 10.6 us -> none  [the longest x16 10.3 us: scores(): offset + jnp.arange(block_size, dtype=jnp.int32)]
    dynamic_slice x16 -> x0, local copies, waits for them, and re-layouts: 9.35 us -> none  [attend(): lax.scan(stats_step, (start_max, start_zero, start_zero), (k_blocks, v_bl...]
  transfers between devices with their start and end apart: 5 -> 0, of which waited for: 5 -> 0; matrix products, arithmetic and copies ran while one was open for 1% -> 0% of each run, Pallas kernels for 0% -> 0%
where the time goes in v1:
time: 126 us; the launch traced here: 125 us
  Pallas kernels  114 us (90%)
  local copies, waits for them, and re-layouts  10.3 us (8%)
    pallas_call x1, Pallas kernels, local_step(): pl.pallas_call(kernel, out_shape=(jax.ShapeDtypeStruct((QL, GROUP * HD),...  114 us
    reshape x1, local copies, waits for them, and re-layouts, local_step(): w_kv.reshape(320, 2, LANES, HD).transpose(0, 2, 1, 3)  4.27 us
    unnamed x5, local copies, waits for them, and re-layouts  4.16 us

profile of v1, /device:TPU:1, one launch (start us, length us, event | category | flops | bytes accessed | tf_op | source)
XLA Modules:
  0.0 125.1 jit_solution(5848861506951497565)
XLA Ops:
  0.6 1.6 %copy.11 = bf16[32,8,2,128]{3,1,2,0:T(8,128)(2,1)} copy(bf16[32,8,2,128]{3,2,1,0:T(2,128)(2,1)} %bitcast.15) | data formatting | bytes 262144
  2.2 4.3 %reshape.20.w_ref = bf16[320,2048]{1,0:T(8,128)(2,1)} reshape(bf16[320,8,2,128]{3,2,1,0:T(2,128)(2,1)} %bitcast.10) | data formatting | bytes 2621440 | tf_op jit(solution)/shard_map/reshape | solution.py:351
  6.5 114.2 %step.1 = (bf16[384,640]{1,0:T(8,128)(2,1)}, bf16[32,5120]{1,0:T(8,128)(2,1)}, f32[320,256]{1,0:T(8,128)}) custom-call(bf16[384,640]{1,0:T(8,128)(2,1)} %bitcast.12, bf16[384,640]{1,0:T(8,128)(2,1)} %bitcast.13, bf16[256,256]{1,0:T(8,128)(2,1)} %bitcast.11, bf16[256,5120]{1,0:T(8,128)(2,1)} %x_ref.1, bf16[320,2048]{1,0:T(8,128)(2,1)} %reshape.20.w_ref), custom_call_target="tpu_custom_call" | custom-call | tf_op jit(solution)/shard_map/step/pallas_call | solution.py:357
  120.6 0.0 copy-start
  120.7 1.9 %reshape.21 = f32[320,2,128]{2,1,0:T(2,128)} reshape(f32[320,256]{1,0:T(8,128)} %get-tuple-element.8) | data formatting | bytes 655360 | tf_op jit(solution)/shard_map/reshape | solution.py:397
  122.6 1.8 %copy.14 = bf16[1,384,640]{2,1,0:T(8,128)(2,1)} copy(bf16[1,384,640]{2,1,0:T(8,128)(2,1)} %bitcast.14) | data formatting | bytes 983040
  124.4 0.0 copy-done
  124.4 0.7 copy.15
Async XLA Ops:
  120.6 3.8 %copy-start = (bf16[32,5120]{1,0:T(8,128)(2,1)S(1)}, bf16[32,5120]{1,0:T(8,128)(2,1)}, u32[]{:S(2)}) copy-start(bf16[32,5120]{1,0:T(8,128)(2,1)} %get-tuple-element.13) | copy-start | bytes 983044
